TPU v7x, 32 devices: a whole 2x2x4 slice. The times are simulated.
32 devices in a mesh: tile: 8 (over z, y), view: 4 (over x, core).
Axes of the slice: x: 2, y: 2, z: 4, core: 2. Of those that a mesh axis runs over, the one named last changes fastest.
Arguments:
- recorded: bfloat16 [4, 128, 256, 256], P('view', 'tile'), may hold values from 0.099609375 to 10
- estimate: float32 [128, 256, 256], P('tile', 'view'), may hold values from 0.5 to 2
- psf_taps: float32 [16, 3, 31], replicated, may hold values from 0.05 to 1
- half_width: int32 [16, 3], replicated, may hold values from 8 to 15
- assign: int32 [4], replicated, may hold values from 0 to 15
- flags: int32 [16, 32], P('tile', 'view'), may hold values 0 or 1
Outputs:
- restored: float32 [128, 256, 256], P('tile', 'view')
All inputs are finite; a program needn't handle non-finite values. No bound on the sum of `flags` on one device may be relied on, other than what follows from the above.
Results may differ from a plain program's by a relative error of at most 0.0007.
Values may be sent and summed in bfloat16 or wider, within the bound.
A program may use at most 64 MiB of HBM per device.

v0:
```python
import jax
import jax.numpy as jnp
from jax import lax
from jax.sharding import PartitionSpec as P

VIEWS = 4
KERNELS = 16
TAPS = 31


def padded_2(cells, sides, width):
    for axis, dim in sides:
        count = lax.axis_size(axis)
        ends = count - 1
        head = lax.slice_in_dim(cells, 0, width, axis=dim)
        tail = lax.slice_in_dim(cells, cells.shape[dim] - width, cells.shape[dim], axis=dim)
        cells = jnp.concatenate(
            [
                lax.ppermute(tail, axis, [(i, (i + 1) % count) for i in range(ends)]),
                cells,
                lax.ppermute(head, axis, [((i + 1) % count, i) for i in range(ends)]),
            ],
            axis=dim,
        )
    return cells


def make_kernels(psf_taps, half_width, assign):
    offsets = jnp.abs(jnp.arange(TAPS) - TAPS // 2)
    keep = (offsets[None, None, :] <= half_width[:, :, None]).astype(jnp.float32)
    raw = psf_taps * keep
    kern = raw / jnp.sum(raw, axis=-1, keepdims=True)
    picker = (assign[:, None] == jnp.arange(KERNELS)[None, :]).astype(jnp.float32)
    return jnp.einsum("sv,vaj->saj", picker, kern, precision=lax.Precision.HIGHEST)


def band_matrix(kernel, rows_count, cols_count, shift):
    rows = jnp.arange(rows_count)[:, None]
    cols = jnp.arange(cols_count)[None, :]
    offset = rows - cols + shift
    hits = (offset[None, :, :] == jnp.arange(TAPS)[:, None, None]).astype(jnp.float32)
    return jnp.sum(kernel[:, None, None] * hits, axis=0)


def along_second(volume, band):
    return jnp.einsum("xpz,pi->xiz", volume, band, precision=lax.Precision.HIGHEST)


def along_third(volume, band):
    return jnp.einsum("xyp,pi->xyi", volume, band, precision=lax.Precision.HIGHEST)


def shards(recorded, estimate, psf_taps, half_width, assign, flags):
    slab = estimate.shape[0]
    full_y = recorded.shape[2]
    depth_z = recorded.shape[3]
    kernels = make_kernels(psf_taps, half_width, assign)
    flipped = kernels[:, :, ::-1]
    slot = lax.axis_index("view")
    selector = (jnp.arange(VIEWS) == slot).astype(jnp.float32)
    own_kern = jnp.einsum("s,saj->aj", selector, kernels, precision=lax.Precision.HIGHEST)
    own_flip = jnp.einsum("s,saj->aj", selector, flipped, precision=lax.Precision.HIGHEST)
    padded_rows = slab + TAPS - 1
    first_own_flip = band_matrix(own_flip[0], padded_rows, slab, 0)
    second_own = band_matrix(own_kern[1], full_y, full_y, TAPS // 2)
    third_own = band_matrix(own_kern[2], depth_z, depth_z, TAPS // 2)
    second_flip = band_matrix(own_flip[1], full_y, full_y, TAPS // 2)
    third_flip = band_matrix(own_flip[2], depth_z, depth_z, TAPS // 2)
    first_all = jnp.stack([band_matrix(kernels[s, 0], padded_rows, slab, 0) for s in range(VIEWS)])
    cells = jnp.repeat(jnp.repeat(flags, 8, axis=0), 8, axis=1)[:, :, None] > 0
    data_slab = recorded[0].astype(jnp.float32)
    current = estimate
    rounded = current.astype(jnp.bfloat16)
    padded = padded_2(rounded, (("tile", 0),), TAPS // 2).astype(jnp.float32)
    stacked = jnp.einsum("pyz,spi->siyz", padded, first_all, precision=lax.Precision.HIGHEST)
    first_pass = lax.all_to_all(
        stacked.astype(jnp.bfloat16), "view", split_axis=0, concat_axis=2, tiled=True
    ).astype(stacked.dtype)[0]
    blurred = along_third(along_second(first_pass, second_own), third_own)
    ratio = (data_slab / blurred).astype(jnp.bfloat16)
    padded_ratio = padded_2(ratio, (("tile", 0),), TAPS // 2).astype(jnp.float32)
    back = jnp.einsum("pyz,pi->iyz", padded_ratio, first_own_flip, precision=lax.Precision.HIGHEST)
    back = along_third(along_second(back, second_flip), third_flip)
    total = lax.psum_scatter(back, "view", scatter_dimension=1, tiled=True)
    correction = total / VIEWS
    current = jnp.where(cells, current * correction, current)
    return current


def solution(mesh):
    placed = (
        P("view", "tile", None, None),
        P("tile", "view", None),
        P(),
        P(),
        P(),
        P("tile", "view"),
    )
    return jax.shard_map(
        shards, mesh=mesh, in_specs=placed, out_specs=P("tile", "view", None), check_vma=False
    )
```

profile of v0, /device:TPU:0, one launch (start us, length us, event | category | flops | bytes accessed | tf_op | source)
XLA Modules:
  0.0 236.5 jit_solution(3409513282182263963)
XLA Ops:
  6.5 1.8 copy.35
  8.6 4.9 %collective-permute-start = (bf16[15,64,256]{2,0,1:T(8,128)(2,1)S(1)}, bf16[15,64,256]{2,0,1:T(8,128)(2,1)S(1)}, u32[]{:S(2)}, u32[]{:S(2)}) collective-permute-start(bf16[15,64,256]{2,0,1:T(8,128)(2,1)S(1)} %get-tuple-element.16), channel_id=1, source_target_pairs={{0,4},{4,8},{8,12},{12,16},{16,20},{20,24},{24,28},{1,5},{5,9},{9,... | collective-permute-start | bytes 1474568 | tf_op jit(solution)/shard_map/ppermute | solution.py:19
  13.5 1.3 collective-permute-start.1
  14.8 0.9 fusion.29
  15.7 0.9 fusion.27
  17.1 0.2 select_reduce_fusion.8
  17.3 18.6 %collective-permute-done = bf16[15,64,256]{2,0,1:T(8,128)(2,1)S(1)} collective-permute-done((bf16[15,64,256]{2,0,1:T(8,128)(2,1)S(1)}, bf16[15,64,256]{2,0,1:T(8,128)(2,1)S(1)}, u32[]{:S(2)}, u32[]{:S(2)}) %collective-permute-start) | collective-permute-done | bytes 491552 | tf_op jit(solution)/shard_map/ppermute | solution.py:19
  35.9 3.2 %convolution_convert_fusion = bf16[4,16,64,256]{3,1,2,0:T(8,128)(2,1)} fusion(bf16[15,64,256]{2,0,1:T(8,128)(2,1)S(1)} %collective-permute-done.1, bf16[16,64,256]{2,0,1:T(8,128)(2,1)S(1)} %copy.35, bf16[15,64,256]{2,0,1:T(8,128)(2,1)S(1)} %collective-permute-done, f32[1,46,16]{1,2,0:T(8,128)S(1)} %bitcast.83, f32[1,46,16]{1,2,0:T(8,128)S(1)} %bitcast.84, ...), kind=kOutput, calls=%fused_computation.18 | convolution fusion | flops 584393344 | bytes 3616256 | tf_op jit(solution)/shard_map/pyz,spi->siyz/dot_general | solution.py:75
  39.0 3.6 %all-to-all-start = ((bf16[4,16,64,256]{3,1,2,0:T(8,128)(2,1)}), bf16[4,16,64,256]{3,1,2,0:T(8,128)(2,1)S(1)}, u32[]{:S(2)}, u32[]{:S(2)}) async-start(bf16[4,16,64,256]{3,1,2,0:T(8,128)(2,1)} %convolution_convert_fusion), calls=%async_computation | async-start | bytes 4194304 | tf_op jit(solution)/shard_map/all_to_all | solution.py:76
  42.7 3.6 %select_reduce_fusion = (f32[256,256]{1,0:T(8,128)S(1)}, f32[256,256]{1,0:T(8,128)S(1)}, f32[256,256]{1,0:T(8,128)S(1)}, f32[256,256]{1,0:T(8,128)S(1)}) fusion(f32[31]{0:T(128)S(1)} %get-tuple-element.28, s32[256,256]{1,0:T(8,128)S(1)} %subtract_add_fusion, f32[31]{0:T(128)S(1)} %get-tuple-element.26, f32[31]{0:T(128)S(1)} %get-tuple-element.25, ...), kind=kLoop, calls=%fused_computation | loop fusion | flops 18022400 | bytes 1311216 | tf_op jit(solution)/shard_map/reduce_sum | solution.py:42
  46.4 21.9 %all-to-all-done = bf16[4,16,64,256]{3,1,2,0:T(8,128)(2,1)S(1)} async-done(((bf16[4,16,64,256]{3,1,2,0:T(8,128)(2,1)}), bf16[4,16,64,256]{3,1,2,0:T(8,128)(2,1)S(1)}, u32[]{:S(2)}, u32[]{:S(2)}) %all-to-all-start) | async-done | bytes 2097184 | tf_op jit(solution)/shard_map/all_to_all | solution.py:76
  68.3 2.2 fusion.9
  70.5 3.7 %fusion.2 = bf16[16,256,256]{2,1,0:T(8,128)(2,1)S(1)} fusion(bf16[1,16,256,256]{3,2,1,0:T(8,128)(2,1)S(1)} %copy-done.1, f32[256,16,256]{2,0,1:T(8,128)S(1)} %fusion.9, f32[256,256]{1,0:T(8,128)S(1)} %get-tuple-element.6), kind=kOutput, calls=%fused_computation.9 | convolution fusion | flops 3224371200 | bytes 8650752 | tf_op jit(solution)/shard_map/xyp,pi->xyi/dot_general | solution.py:50
  74.2 0.4 fusion.51
  74.6 4.5 %collective-permute-start.2 = (bf16[15,256,256]{2,1,0:T(8,128)(2,1)S(1)}, bf16[15,256,256]{2,1,0:T(8,128)(2,1)S(1)}, u32[]{:S(2)}, u32[]{:S(2)}) collective-permute-start(bf16[15,256,256]{2,1,0:T(8,128)(2,1)S(1)} %get-tuple-element.14), channel_id=1, source_target_pairs={{0,4},{4,8},{8,12},{12,16},{16,20},{20,24},{24,28},{1,5},{5,9},{9,... | collective-permute-start | bytes 5898248 | tf_op jit(solution)/shard_map/ppermute | solution.py:19
  79.1 1.5 collective-permute-start.3
  80.6 82.3 %collective-permute-done.2 = bf16[15,256,256]{2,1,0:T(8,128)(2,1)S(1)} collective-permute-done((bf16[15,256,256]{2,1,0:T(8,128)(2,1)S(1)}, bf16[15,256,256]{2,1,0:T(8,128)(2,1)S(1)}, u32[]{:S(2)}, u32[]{:S(2)}) %collective-permute-start.2) | collective-permute-done | bytes 1966112 | tf_op jit(solution)/shard_map/ppermute | solution.py:19
  162.9 0.9 pad_maximum_fusion
  163.8 5.3 %fusion = f32[16,256,256]{2,0,1:T(8,128)S(1)} fusion(bf16[46,256,256]{2,1,0:T(8,128)(2,1)S(1)} %pad_maximum_fusion, f32[46,16]{0,1:T(8,128)S(1)} %get-tuple-element.9), kind=kOutput, calls=%fused_computation.5 | convolution fusion | flops 578813952 | bytes 10226560 | tf_op jit(solution)/shard_map/pyz,pi->iyz/dot_general | solution.py:82
  169.1 6.3 %fusion.7 = f32[256,16,256]{2,0,1:T(8,128)S(1)} fusion(f32[16,256,256]{2,0,1:T(8,128)S(1)} %fusion, f32[256,256]{1,0:T(8,128)S(1)} %get-tuple-element.8), kind=kOutput, calls=%fused_computation.14 | convolution fusion | flops 3221225472 | bytes 8650752 | tf_op jit(solution)/shard_map/xpz,pi->xiz/dot_general | solution.py:46
  175.4 5.0 %fusion.3 = f32[16,256,256]{2,1,0:T(8,128)} fusion(f32[256,16,256]{2,0,1:T(8,128)S(1)} %fusion.7, f32[256,256]{1,0:T(8,128)S(1)} %get-tuple-element.5), kind=kOutput, calls=%fused_computation.10 | convolution fusion | flops 3221225472 | bytes 8650752 | tf_op jit(solution)/shard_map/xyp,pi->xyi/dot_general | solution.py:50
  180.4 0.7 copy-done.2
  181.2 46.1 %reduce-scatter.2.cloned.1.call-done = f32[16,64,256]{2,1,0:T(8,128)} async-done(((f32[16,256,256]{2,1,0:T(8,128)}), f32[16,64,256]{2,1,0:T(8,128)}) %reduce-scatter.2.cloned.1.call-update) | async-done | bytes 1048592 | tf_op jit(solution)/shard_map/reduce_scatter | solution.py:84
  227.3 2.4 %multiply_select_fusion = f32[16,64,256]{2,1,0:T(8,128)} fusion(f32[16,64,256]{2,1,0:T(8,128)S(1)} %copy-done, f32[16,64,256]{2,1,0:T(8,128)} %reduce-scatter.2.cloned.1.call-done, pred[16,64]{1,0:T(8,128)(4,1)S(1)} %copy.12), kind=kLoop, calls=%fused_computation.24 | loop fusion | flops 786432 | bytes 3146752 | tf_op jit(solution)/shard_map/jit(_where)/select_n | solution.py:86
  (25 shorter events, 0.9 us)
Async XLA Ops:
  8.6 27.3 %collective-permute-start = (bf16[15,64,256]{2,0,1:T(8,128)(2,1)S(1)}, bf16[15,64,256]{2,0,1:T(8,128)(2,1)S(1)}, u32[]{:S(2)}, u32[]{:S(2)}) collective-permute-start(bf16[15,64,256]{2,0,1:T(8,128)(2,1)S(1)} %get-tuple-element.16), channel_id=1, source_target_pairs={{0,4},{4,8},{8,12},{12,16},{16,20},{20,24},{24,28},{1,5},{5,9},{9,... | collective-permute-start | bytes 1474568 | tf_op jit(solution)/shard_map/ppermute | solution.py:19
  13.5 22.4 %collective-permute-start.1 = (bf16[15,64,256]{2,0,1:T(8,128)(2,1)S(1)}, bf16[15,64,256]{2,0,1:T(8,128)(2,1)S(1)}, u32[]{:S(2)}, u32[]{:S(2)}) collective-permute-start(bf16[15,64,256]{2,0,1:T(8,128)(2,1)S(1)} %get-tuple-element.17), channel_id=1, source_target_pairs={{4,0},{8,4},{12,8},{16,12},{20,16},{24,20},{28,24},{5,1},{9,5},{13... | collective-permute-start | bytes 1474568 | tf_op jit(solution)/shard_map/ppermute | solution.py:21
  39.0 29.2 %all-to-all-start = ((bf16[4,16,64,256]{3,1,2,0:T(8,128)(2,1)}), bf16[4,16,64,256]{3,1,2,0:T(8,128)(2,1)S(1)}, u32[]{:S(2)}, u32[]{:S(2)}) async-start(bf16[4,16,64,256]{3,1,2,0:T(8,128)(2,1)} %convolution_convert_fusion), calls=%async_computation | async-start | bytes 4194304 | tf_op jit(solution)/shard_map/all_to_all | solution.py:76
  42.6 184.7 %reduce-scatter.2.cloned.1.call-start = ((), (), s32[]{:S(2)}) async-start(), calls=%async_computation.2 | async-start | bytes 5242880 | tf_op jit(solution)/shard_map/reduce_scatter | solution.py:84
  68.3 2.2 copy-start.1
  74.6 88.3 %collective-permute-start.2 = (bf16[15,256,256]{2,1,0:T(8,128)(2,1)S(1)}, bf16[15,256,256]{2,1,0:T(8,128)(2,1)S(1)}, u32[]{:S(2)}, u32[]{:S(2)}) collective-permute-start(bf16[15,256,256]{2,1,0:T(8,128)(2,1)S(1)} %get-tuple-element.14), channel_id=1, source_target_pairs={{0,4},{4,8},{8,12},{12,16},{16,20},{20,24},{24,28},{1,5},{5,9},{9,... | collective-permute-start | bytes 5898248 | tf_op jit(solution)/shard_map/ppermute | solution.py:19
  79.1 83.8 %collective-permute-start.3 = (bf16[15,256,256]{2,1,0:T(8,128)(2,1)S(1)}, bf16[15,256,256]{2,1,0:T(8,128)(2,1)S(1)}, u32[]{:S(2)}, u32[]{:S(2)}) collective-permute-start(bf16[15,256,256]{2,1,0:T(8,128)(2,1)S(1)} %get-tuple-element.15), channel_id=1, source_target_pairs={{4,0},{8,4},{12,8},{16,12},{20,16},{24,20},{28,24},{5,1},{9,5},{13... | collective-permute-start | bytes 5898248 | tf_op jit(solution)/shard_map/ppermute | solution.py:21
  180.3 0.7 copy-start.2
  180.3 47.0 %copy-start = (f32[16,64,256]{2,1,0:T(8,128)S(1)}, f32[16,64,256]{2,1,0:T(8,128)}, u32[]{:S(2)}) copy-start(f32[16,64,256]{2,1,0:T(8,128)} %param.7) | copy-start | bytes 3145732
Sparse Core Ops, SparseCore 0:
  180.5 46.7 reduce-scatter.1
where the time goes:
time: 237 us
  waiting for transfers between devices  169 us (71%)
  matrix products  26.7 us (11%)
  starting transfers between devices  15.9 us (7%)
  between operations  13.6 us (6%)
  other arithmetic  8.14 us (3%)
  local copies, waits for them, and re-layouts  3.41 us (1%)
    ppermute x2, waiting for transfers between devices, padded_2(): lax.ppermute(tail, axis, [(i, (i + 1) % count) for i in range(ends)])  101 us
    reduce_scatter x1, waiting for transfers between devices, shards(): total = lax.psum_scatter(back, 'view', scatter_dimension=1, tiled=True)  46.1 us
    all_to_all x1, waiting for transfers between devices, shards(): lax.all_to_all(stacked.astype(jnp.bfloat16), 'view', split_axis=0, concat...  21.9 us
    ppermute x2, starting transfers between devices, padded_2(): lax.ppermute(tail, axis, [(i, (i + 1) % count) for i in range(ends)])  9.45 us
    dot_general x2, matrix products, along_third(): jnp.einsum('xyp,pi->xyi', volume, band, precision=lax.Precision.HIGHEST)  8.62 us
    dot_general x2, matrix products, along_second(): jnp.einsum('xpz,pi->xiz', volume, band, precision=lax.Precision.HIGHEST)  8.45 us
    dot_general x1, matrix products, shards(): jnp.einsum('pyz,pi->iyz', padded_ratio, first_own_flip, precision=lax.Pre...  5.27 us
  transfers between devices with their start and end apart: 6, of which 4 were waited for; matrix products, arithmetic and copies ran while one was open for 3% of the time, Pallas kernels for 0%

commit v1 on v0

--- a/solution.py
+++ b/solution.py
@@ -6,6 +6,36 @@
 VIEWS = 4
 KERNELS = 16
 TAPS = 31
+
+
+def render_the_seats_all(panel, dim_k, my_data):
+    f_now = panel.shape
+    newest = panel.reshape(*f_now[:dim_k], my_data, f_now[dim_k] // my_data, *f_now[dim_k + 1 :])
+    z = jnp.moveaxis(newest, dim_k, 0)
+    return z
+
+
+def _fix_run(field_in, dim_at):
+    big = list(field_in.shape[1:])
+    big[dim_at] *= field_in.shape[0]
+    s_next = jnp.moveaxis(field_in, 0, dim_at).reshape(big)
+    return s_next
+
+
+def compute_the_ladders(frame, across, mine_x, state):
+    v1 = lax.psum(1, across)
+    w_next, block_next = (v1, lax.axis_index(across))
+    y1 = render_the_seats_all(frame, mine_x, w_next)
+    pile = [y1[block_next]]
+    for j in range(1, w_next):
+        current_value = y1[(block_next + j) % w_next]
+        small = lax.ppermute(
+            current_value, across, [(at, (at + j) % w_next) for at in range(w_next)]
+        )
+        pile.append(small)
+    y1 = jnp.stack(pile, axis=0)[(block_next - jnp.arange(w_next)) % w_next]
+    left_arr = _fix_run(y1, state)
+    return left_arr
 
 
 def padded_2(cells, sides, width):
@@ -73,9 +103,9 @@
     rounded = current.astype(jnp.bfloat16)
     padded = padded_2(rounded, (("tile", 0),), TAPS // 2).astype(jnp.float32)
     stacked = jnp.einsum("pyz,spi->siyz", padded, first_all, precision=lax.Precision.HIGHEST)
-    first_pass = lax.all_to_all(
-        stacked.astype(jnp.bfloat16), "view", split_axis=0, concat_axis=2, tiled=True
-    ).astype(stacked.dtype)[0]
+    first_pass = compute_the_ladders(stacked.astype(jnp.bfloat16), "view", 0, 2).astype(
+        stacked.dtype
+    )[0]
     blurred = along_third(along_second(first_pass, second_own), third_own)
     ratio = (data_slab / blurred).astype(jnp.bfloat16)
     padded_ratio = padded_2(ratio, (("tile", 0),), TAPS // 2).astype(jnp.float32)

time: 237 us -> 236 us (level)
  local copies, waits for them, and re-layouts: 3.41 us -> 5.88 us
    all_to_all x1 -> x0, waiting for transfers between devices: 21.9 us -> none  [shards(): lax.all_to_all(stacked.astype(jnp.bfloat16), 'view', split_axis=0, concat...]
    ppermute x0 -> x3, waiting for transfers between devices: none -> 17.9 us  [compute_the_ladders(): lax.ppermute(current_value, across, [(at, (at + j) % w_next) for at in ra...]
    all_to_all x1 -> x0, starting transfers between devices: 3.61 us -> none  [shards(): lax.all_to_all(stacked.astype(jnp.bfloat16), 'view', split_axis=0, concat...]
    ppermute x0 -> x3, starting transfers between devices: none -> 3 us  [compute_the_ladders(): lax.ppermute(current_value, across, [(at, (at + j) % w_next) for at in ra...]
    ppermute x2, waiting for transfers between devices: 101 us -> 103 us  [padded_2(): lax.ppermute(tail, axis, [(i, (i + 1) % count) for i in range(ends)])]
  transfers between devices with their start and end apart: 6 -> 8, of which waited for: 4 -> 6; matrix products, arithmetic and copies ran while one was open for 3% -> 2% of each run, Pallas kernels for 0% -> 0%
where the time goes in v1:
time: 236 us
  waiting for transfers between devices  167 us (71%)
  matrix products  24.6 us (10%)
  starting transfers between devices  15.2 us (6%)
  between operations  13.7 us (6%)
  other arithmetic  9.02 us (4%)
  local copies, waits for them, and re-layouts  5.88 us (2%)
    ppermute x2, waiting for transfers between devices, padded_2(): lax.ppermute(tail, axis, [(i, (i + 1) % count) for i in range(ends)])  103 us
    reduce_scatter x1, waiting for transfers between devices, shards(): total = lax.psum_scatter(back, 'view', scatter_dimension=1, tiled=True)  46 us
    ppermute x3, waiting for transfers between devices, compute_the_ladders(): lax.ppermute(current_value, across, [(at, (at + j) % w_next) for at in ra...  17.9 us
    ppermute x2, starting transfers between devices, padded_2(): lax.ppermute(tail, axis, [(i, (i + 1) % count) for i in range(ends)])  9.44 us
    dot_general x2, matrix products, along_third(): jnp.einsum('xyp,pi->xyi', volume, band, precision=lax.Precision.HIGHEST)  8.61 us
    dot_general x2, matrix products, along_second(): jnp.einsum('xpz,pi->xiz', volume, band, precision=lax.Precision.HIGHEST)  8.45 us
    dot_general x1, matrix products, shards(): jnp.einsum('pyz,pi->iyz', padded_ratio, first_own_flip, precision=lax.Pre...  5.27 us
  transfers between devices with their start and end apart: 8, of which 6 were waited for; matrix products, arithmetic and copies ran while one was open for 2% of the time, Pallas kernels for 0%

profile of v1, /device:TPU:0, one launch (start us, length us, event | category | flops | bytes accessed | tf_op | source)
XLA Modules:
  0.0 235.7 jit_solution(6731506186799451247)
XLA Ops:
  6.5 1.8 copy.35
  8.6 4.9 %collective-permute-start = (bf16[15,64,256]{2,0,1:T(8,128)(2,1)S(1)}, bf16[15,64,256]{2,0,1:T(8,128)(2,1)S(1)}, u32[]{:S(2)}, u32[]{:S(2)}) collective-permute-start(bf16[15,64,256]{2,0,1:T(8,128)(2,1)S(1)} %get-tuple-element.20), channel_id=1, source_target_pairs={{0,4},{4,8},{8,12},{12,16},{16,20},{20,24},{24,28},{1,5},{5,9},{9,... | collective-permute-start | bytes 1474568 | tf_op jit(solution)/shard_map/ppermute | solution.py:49
  13.5 1.3 collective-permute-start.1
  16.0 19.9 %collective-permute-done = bf16[15,64,256]{2,0,1:T(8,128)(2,1)S(1)} collective-permute-done((bf16[15,64,256]{2,0,1:T(8,128)(2,1)S(1)}, bf16[15,64,256]{2,0,1:T(8,128)(2,1)S(1)}, u32[]{:S(2)}, u32[]{:S(2)}) %collective-permute-start) | collective-permute-done | bytes 491552 | tf_op jit(solution)/shard_map/ppermute | solution.py:49
  35.9 1.8 convolution_convert_fusion
  37.9 1.6 collective-permute-start.3
  39.5 1.4 collective-permute-start.4
  40.9 3.6 %select_reduce_fusion = (f32[256,256]{1,0:T(8,128)S(1)}, f32[256,256]{1,0:T(8,128)S(1)}, f32[256,256]{1,0:T(8,128)S(1)}, f32[256,256]{1,0:T(8,128)S(1)}) fusion(f32[31]{0:T(128)S(1)} %get-tuple-element.32, s32[256,256]{1,0:T(8,128)S(1)} %subtract_add_fusion, f32[31]{0:T(128)S(1)} %get-tuple-element.30, f32[31]{0:T(128)S(1)} %get-tuple-element.29, ...), kind=kLoop, calls=%fused_computation.1 | loop fusion | flops 18022400 | bytes 1311216 | tf_op jit(solution)/shard_map/reduce_sum | solution.py:72
  44.5 7.0 %collective-permute-done.2 = bf16[1,16,64,256]{3,1,2,0:T(8,128)(2,1)S(1)} collective-permute-done((bf16[1,16,64,256]{3,1,2,0:T(8,128)(2,1)S(1)}, bf16[1,16,64,256]{3,1,2,0:T(8,128)(2,1)S(1)}, u32[]{:S(2)}, u32[]{:S(2)}) %collective-permute-start.2) | collective-permute-done | bytes 524320 | tf_op jit(solution)/shard_map/ppermute | solution.py:32
  51.5 1.3 collective-permute-done.3
  52.8 9.6 %collective-permute-done.4 = bf16[1,16,64,256]{3,1,2,0:T(8,128)(2,1)S(1)} collective-permute-done((bf16[1,16,64,256]{3,1,2,0:T(8,128)(2,1)S(1)}, bf16[1,16,64,256]{3,1,2,0:T(8,128)(2,1)S(1)}, u32[]{:S(2)}, u32[]{:S(2)}) %collective-permute-start.4) | collective-permute-done | bytes 524320 | tf_op jit(solution)/shard_map/ppermute | solution.py:32
  62.4 1.6 maximum_bitcast_fusion
  64.0 2.3 gather_fusion
  66.3 2.2 fusion.9
  68.5 3.7 %fusion.2 = bf16[16,256,256]{2,1,0:T(8,128)(2,1)S(1)} fusion(bf16[1,16,256,256]{3,2,1,0:T(8,128)(2,1)S(1)} %copy-done.3, f32[256,16,256]{2,0,1:T(8,128)S(1)} %fusion.9, f32[256,256]{1,0:T(8,128)S(1)} %get-tuple-element.6), kind=kOutput, calls=%fused_computation.10 | convolution fusion | flops 3224371200 | bytes 8650752 | tf_op jit(solution)/shard_map/xyp,pi->xyi/dot_general | solution.py:80
  72.6 4.5 %collective-permute-start.5 = (bf16[15,256,256]{2,1,0:T(8,128)(2,1)S(1)}, bf16[15,256,256]{2,1,0:T(8,128)(2,1)S(1)}, u32[]{:S(2)}, u32[]{:S(2)}) collective-permute-start(bf16[15,256,256]{2,1,0:T(8,128)(2,1)S(1)} %get-tuple-element.14), channel_id=1, source_target_pairs={{0,4},{4,8},{8,12},{12,16},{16,20},{20,24},{24,28},{1,5},{5,9},{9,... | collective-permute-start | bytes 5898248 | tf_op jit(solution)/shard_map/ppermute | solution.py:49
  77.1 1.5 collective-permute-start.6
  78.6 83.6 %collective-permute-done.5 = bf16[15,256,256]{2,1,0:T(8,128)(2,1)S(1)} collective-permute-done((bf16[15,256,256]{2,1,0:T(8,128)(2,1)S(1)}, bf16[15,256,256]{2,1,0:T(8,128)(2,1)S(1)}, u32[]{:S(2)}, u32[]{:S(2)}) %collective-permute-start.5) | collective-permute-done | bytes 1966112 | tf_op jit(solution)/shard_map/ppermute | solution.py:49
  162.2 0.9 pad_maximum_fusion
  163.1 5.3 %fusion = f32[16,256,256]{2,0,1:T(8,128)S(1)} fusion(bf16[46,256,256]{2,1,0:T(8,128)(2,1)S(1)} %pad_maximum_fusion, f32[46,16]{0,1:T(8,128)S(1)} %get-tuple-element.9), kind=kOutput, calls=%fused_computation.6 | convolution fusion | flops 578813952 | bytes 10226560 | tf_op jit(solution)/shard_map/pyz,pi->iyz/dot_general | solution.py:112
  168.4 6.3 %fusion.7 = f32[256,16,256]{2,0,1:T(8,128)S(1)} fusion(f32[16,256,256]{2,0,1:T(8,128)S(1)} %fusion, f32[256,256]{1,0:T(8,128)S(1)} %get-tuple-element.8), kind=kOutput, calls=%fused_computation.15 | convolution fusion | flops 3221225472 | bytes 8650752 | tf_op jit(solution)/shard_map/xpz,pi->xiz/dot_general | solution.py:76
  174.7 5.0 %fusion.3 = f32[16,256,256]{2,1,0:T(8,128)} fusion(f32[256,16,256]{2,0,1:T(8,128)S(1)} %fusion.7, f32[256,256]{1,0:T(8,128)S(1)} %get-tuple-element.5), kind=kOutput, calls=%fused_computation.11 | convolution fusion | flops 3221225472 | bytes 8650752 | tf_op jit(solution)/shard_map/xyp,pi->xyi/dot_general | solution.py:80
  180.5 46.0 %reduce-scatter.2.cloned.1.call-done = f32[16,64,256]{2,1,0:T(8,128)} async-done(((f32[16,256,256]{2,1,0:T(8,128)}), f32[16,64,256]{2,1,0:T(8,128)}) %reduce-scatter.2.cloned.1.call-update) | async-done | bytes 1048592 | tf_op jit(solution)/shard_map/reduce_scatter | solution.py:114
  226.4 2.4 %multiply_select_fusion = f32[16,64,256]{2,1,0:T(8,128)} fusion(f32[16,64,256]{2,1,0:T(8,128)S(1)} %copy-done, f32[16,64,256]{2,1,0:T(8,128)} %reduce-scatter.2.cloned.1.call-done, pred[16,64]{1,0:T(8,128)(4,1)S(1)} %copy.12), kind=kLoop, calls=%fused_computation.26 | loop fusion | flops 786432 | bytes 3146752 | tf_op jit(solution)/shard_map/jit(_where)/select_n | solution.py:116
  (40 shorter events, 2.8 us)
Async XLA Ops:
  6.5 8.3 %copy-start.1 = (f32[16,3,31]{2,0,1:T(8,128)S(1)}, f32[16,3,31]{2,0,1:T(8,128)}, u32[]{:S(2)}) copy-start(f32[16,3,31]{2,0,1:T(8,128)} %param.8) | copy-start | bytes 17860
  6.5 8.3 %copy-start.2 = (s32[16,3]{0,1:T(4,128)S(1)}, s32[16,3]{0,1:T(4,128)}, u32[]{:S(2)}) copy-start(s32[16,3]{0,1:T(4,128)} %param.9) | copy-start | bytes 580
  6.5 8.5 %copy-start.5 = (s32[4]{0:T(128)S(1)}, s32[4]{0:T(128)}, u32[]{:S(2)}) copy-start(s32[4]{0:T(128)} %param.10) | copy-start | bytes 52
  6.5 219.9 %reduce-scatter.2.cloned.1.call-start = ((), (), s32[]{:S(2)}) async-start(), calls=%async_computation.1 | async-start | bytes 5242880 | tf_op jit(solution)/shard_map/reduce_scatter | solution.py:114
  8.6 27.3 %collective-permute-start = (bf16[15,64,256]{2,0,1:T(8,128)(2,1)S(1)}, bf16[15,64,256]{2,0,1:T(8,128)(2,1)S(1)}, u32[]{:S(2)}, u32[]{:S(2)}) collective-permute-start(bf16[15,64,256]{2,0,1:T(8,128)(2,1)S(1)} %get-tuple-element.20), channel_id=1, source_target_pairs={{0,4},{4,8},{8,12},{12,16},{16,20},{20,24},{24,28},{1,5},{5,9},{9,... | collective-permute-start | bytes 1474568 | tf_op jit(solution)/shard_map/ppermute | solution.py:49
  13.5 22.4 %collective-permute-start.1 = (bf16[15,64,256]{2,0,1:T(8,128)(2,1)S(1)}, bf16[15,64,256]{2,0,1:T(8,128)(2,1)S(1)}, u32[]{:S(2)}, u32[]{:S(2)}) collective-permute-start(bf16[15,64,256]{2,0,1:T(8,128)(2,1)S(1)} %get-tuple-element.21), channel_id=1, source_target_pairs={{4,0},{8,4},{12,8},{16,12},{20,16},{24,20},{28,24},{5,1},{9,5},{13... | collective-permute-start | bytes 1474568 | tf_op jit(solution)/shard_map/ppermute | solution.py:51
  37.9 13.6 %collective-permute-start.2 = (bf16[1,16,64,256]{3,1,2,0:T(8,128)(2,1)S(1)}, bf16[1,16,64,256]{3,1,2,0:T(8,128)(2,1)S(1)}, u32[]{:S(2)}, u32[]{:S(2)}) collective-permute-start(bf16[1,16,64,256]{3,1,2,0:T(8,128)(2,1)S(1)} %get-tuple-element.19), channel_id=1, source_target_pairs={{0,1},{1,2},{2,3},{3,0},{4,5},{5,6},{6,7},{7,4},{8,9},{9,10},{10,1... | collective-permute-start | bytes 1572872 | tf_op jit(solution)/shard_map/ppermute | solution.py:32
  37.9 14.9 %collective-permute-start.3 = (bf16[1,16,64,256]{3,1,2,0:T(8,128)(2,1)S(1)}, bf16[1,16,64,256]{3,1,2,0:T(8,128)(2,1)S(1)}, u32[]{:S(2)}, u32[]{:S(2)}) collective-permute-start(bf16[1,16,64,256]{3,1,2,0:T(8,128)(2,1)S(1)} %get-tuple-element.18), channel_id=1, source_target_pairs={{0,2},{1,3},{2,0},{3,1},{4,6},{5,7},{6,4},{7,5},{8,10},{9,11},{10,... | collective-permute-start | bytes 1572872 | tf_op jit(solution)/shard_map/ppermute | solution.py:32
  39.5 22.9 %collective-permute-start.4 = (bf16[1,16,64,256]{3,1,2,0:T(8,128)(2,1)S(1)}, bf16[1,16,64,256]{3,1,2,0:T(8,128)(2,1)S(1)}, u32[]{:S(2)}, u32[]{:S(2)}) collective-permute-start(bf16[1,16,64,256]{3,1,2,0:T(8,128)(2,1)S(1)} %get-tuple-element.17), channel_id=1, source_target_pairs={{0,3},{1,0},{2,1},{3,2},{4,7},{5,4},{6,5},{7,6},{8,11},{9,8},{10,9... | collective-permute-start | bytes 1572872 | tf_op jit(solution)/shard_map/ppermute | solution.py:32
  66.3 2.2 copy-start.3
  72.6 89.6 %collective-permute-start.5 = (bf16[15,256,256]{2,1,0:T(8,128)(2,1)S(1)}, bf16[15,256,256]{2,1,0:T(8,128)(2,1)S(1)}, u32[]{:S(2)}, u32[]{:S(2)}) collective-permute-start(bf16[15,256,256]{2,1,0:T(8,128)(2,1)S(1)} %get-tuple-element.14), channel_id=1, source_target_pairs={{0,4},{4,8},{8,12},{12,16},{16,20},{20,24},{24,28},{1,5},{5,9},{9,... | collective-permute-start | bytes 5898248 | tf_op jit(solution)/shard_map/ppermute | solution.py:49
  77.1 85.0 %collective-permute-start.6 = (bf16[15,256,256]{2,1,0:T(8,128)(2,1)S(1)}, bf16[15,256,256]{2,1,0:T(8,128)(2,1)S(1)}, u32[]{:S(2)}, u32[]{:S(2)}) collective-permute-start(bf16[15,256,256]{2,1,0:T(8,128)(2,1)S(1)} %get-tuple-element.15), channel_id=1, source_target_pairs={{4,0},{8,4},{12,8},{16,12},{20,16},{24,20},{28,24},{5,1},{9,5},{13... | collective-permute-start | bytes 5898248 | tf_op jit(solution)/shard_map/ppermute | solution.py:51
  179.6 0.7 copy-start.4
  179.6 46.8 %copy-start = (f32[16,64,256]{2,1,0:T(8,128)S(1)}, f32[16,64,256]{2,1,0:T(8,128)}, u32[]{:S(2)}) copy-start(f32[16,64,256]{2,1,0:T(8,128)} %param.7) | copy-start | bytes 3145732
Sparse Core Ops, SparseCore 0:
  179.8 46.6 reduce-scatter.1
